TPU v7x, 32 devices: a whole 2x2x4 slice. The times are simulated.
32 devices in a mesh: space: 8 (over y, x, core), src: 4 (over z).
Axes of the slice: x: 2, y: 2, z: 4, core: 2. Of those that a mesh axis runs over, the one named last changes fastest.
Arguments:
- potential_start: float32 [16, 4, 128, 1024], P('src', None, 'space'), may hold values from -6 to 6
- adjoint_start: float32 [16, 4, 128, 1024], P('src', None, 'space'), may hold values from -6 to 6
- conductivity: float32 [4, 128, 1024], P(None, 'space', 'src'), may hold values from 0.1 to 1
- electrodes: int32 [16, 2], P('src'), may hold values from 0 to 131071
- receivers: int32 [16, 32, 2], P('src'), may hold values from 0 to 131071
- observed: float32 [16, 32], P('src'), may hold values from -6 to 6
Outputs:
- gradient: float32 [4, 128, 1024], P(None, 'space', 'src')
Inputs may be any that keep to these rules, and one draw needn't show every extreme that they name: `electrodes`: each entry is a surface node id row * 1024 + column. `receivers`: each entry is a surface node id row * 1024 + column.
All inputs are finite; a program needn't handle non-finite values.
Results may differ from a plain program's by a relative error of at most 0.00002.
Values sent between devices are 32-bit elements; how exact they have to be, the bound alone decides.
No kernel may reach another device: no remote copies, remote signals or barrier semaphores. Data moves between devices by JAX's collectives and lax.ppermute only.
A program may use at most 64 MiB of HBM per device.

v0:
```python
import jax
import jax.numpy as jnp
from jax import lax
from jax.sharding import PartitionSpec as P

SWEEPS = 4
GAMMA = 0.5
CURRENT = 4.0
THETA = 1.025
DELTA = 0.975
RATIO = THETA / DELTA


def padded_2(block, sides, width):
    for axis, dim in sides:
        count = lax.axis_size(axis)
        forward = [(i, i + 1) for i in range(count - 1)]
        backward = [(target, source) for source, target in forward]
        low = lax.ppermute(
            lax.slice_in_dim(block, block.shape[dim] - width, None, axis=dim), axis, forward
        )
        high = lax.ppermute(lax.slice_in_dim(block, 0, width, axis=dim), axis, backward)
        block = jnp.concatenate([low, block, high], axis=dim)
    return block


def pad_axis(field, dimension, margin):
    widths = [(0, 0)] * field.ndim
    widths[dimension % field.ndim] = (margin, margin)
    return jnp.pad(field, widths)


def coefficients(padded_sigma):
    centre_sigma = padded_sigma[:, 1:-1, :]
    layer_pad = pad_axis(centre_sigma, 0, 1)
    column_pad = pad_axis(centre_sigma, 2, 1)
    face_terms = (
        0.5 * (centre_sigma + padded_sigma[:, :-2, :]),
        0.5 * (centre_sigma + padded_sigma[:, 2:, :]),
        0.5 * (centre_sigma + column_pad[:, :, :-2]),
        0.5 * (centre_sigma + column_pad[:, :, 2:]),
        0.5 * (centre_sigma + layer_pad[:-2]),
        0.5 * (centre_sigma + layer_pad[2:]),
    )
    diagonal = (
        face_terms[0]
        + face_terms[1]
        + face_terms[2]
        + face_terms[3]
        + face_terms[4]
        + face_terms[5]
        + GAMMA * centre_sigma
    )
    return (face_terms, diagonal)


def apply_operator(padded, face_terms, diagonal):
    centre = padded[..., 1:-1, :]
    layer_pad = pad_axis(centre, -3, 1)
    column_pad = pad_axis(centre, -1, 1)
    neighbours = (
        face_terms[0] * padded[..., :-2, :]
        + face_terms[1] * padded[..., 2:, :]
        + face_terms[2] * column_pad[..., :-2]
        + face_terms[3] * column_pad[..., 2:]
        + face_terms[4] * layer_pad[..., :-2, :, :]
        + face_terms[5] * layer_pad[..., 2:, :, :]
    )
    return diagonal * centre - neighbours


def chebyshev(initial, source, face_terms, diagonal, inverse, extend, inside_rows):
    residual = source - apply_operator(extend(initial), face_terms, diagonal)
    residual = residual * inside_rows
    direction = inverse * residual / THETA
    factor = 1.0 / RATIO
    potential = initial
    for sweep in range(SWEEPS):
        potential = potential + direction
        if sweep + 1 < SWEEPS:
            residual = residual - apply_operator(extend(direction), face_terms, diagonal)
            residual = residual * inside_rows
            factor_next = 1.0 / (2.0 * RATIO - factor)
            direction = (
                factor_next * factor * direction + 2.0 * factor_next / DELTA * inverse * residual
            )
            factor = factor_next
    return potential


def sensitivity(forward_pad, adjoint_pad):
    forward_mid = forward_pad[..., 1:-1, :]
    adjoint_mid = adjoint_pad[..., 1:-1, :]
    forward_layer = pad_axis(forward_mid, -3, 1)
    adjoint_layer = pad_axis(adjoint_mid, -3, 1)
    forward_column = pad_axis(forward_mid, -1, 1)
    adjoint_column = pad_axis(adjoint_mid, -1, 1)
    pairs = (
        (forward_pad[..., :-2, :], adjoint_pad[..., :-2, :]),
        (forward_pad[..., 2:, :], adjoint_pad[..., 2:, :]),
        (forward_column[..., :-2], adjoint_column[..., :-2]),
        (forward_column[..., 2:], adjoint_column[..., 2:]),
        (forward_layer[..., :-2, :, :], adjoint_layer[..., :-2, :, :]),
        (forward_layer[..., 2:, :, :], adjoint_layer[..., 2:, :, :]),
    )
    running = GAMMA * forward_mid * adjoint_mid
    for forward_near, adjoint_near in pairs:
        running = running + 0.5 * (forward_mid - forward_near) * (adjoint_mid - adjoint_near)
    return -running


def local_pad(field):
    return pad_axis(field, -2, 1)


def surface_source(node_ids, amounts, base_row, span, layer_count, columns):
    sources_here = node_ids.shape[0]
    local_ids = node_ids - base_row * columns
    inside = (local_ids >= 0) & (local_ids < span * columns)
    slots = jnp.clip(local_ids, 0, span * columns - 1)
    source_rows = jnp.broadcast_to(
        jnp.arange(sources_here, dtype=jnp.int32)[:, None], node_ids.shape
    )
    plane = (
        jnp.zeros((sources_here, span * columns), jnp.float32)
        .at[source_rows, slots]
        .add(jnp.where(inside, amounts, 0.0))
    )
    plane = plane.reshape(sources_here, 1, span, columns)
    return jnp.concatenate(
        [plane, jnp.zeros((sources_here, layer_count - 1, span, columns), jnp.float32)], axis=1
    )


def per_device(potential_start, adjoint_start, conductivity, electrodes, receivers, observed):
    sources_here, layer_count, row_count, columns = potential_start.shape
    whole_sigma = lax.all_gather(conductivity, "src", axis=2, tiled=True)
    first_row = lax.axis_index("space") * row_count
    total_rows = row_count * lax.axis_size("space")
    margin_rows = SWEEPS + 1

    def widen(field):
        return padded_2(field, (("space", 2),), margin_rows)

    padded_sigma = padded_2(whole_sigma, (("space", 1),), margin_rows + 1)
    face_terms, diagonal = coefficients(padded_sigma)
    global_rows = first_row - margin_rows + jnp.arange(row_count + 2 * margin_rows, dtype=jnp.int32)
    inside_rows = ((global_rows >= 0) & (global_rows < total_rows)).astype(jnp.float32)[:, None]
    inverse = 1.0 / jnp.where(inside_rows > 0, diagonal, 1.0)
    forward_init = widen(potential_start)
    adjoint_init = widen(adjoint_start)
    span = row_count + 2 * margin_rows
    base_row = first_row - margin_rows
    currents = jnp.broadcast_to(jnp.array([CURRENT, -CURRENT], jnp.float32), electrodes.shape)
    injected = surface_source(electrodes, currents, base_row, span, layer_count, columns)
    forward = chebyshev(
        forward_init, injected, face_terms, diagonal, inverse, local_pad, inside_rows
    )
    surface = forward[:, 0, margin_rows : margin_rows + row_count, :].reshape(
        sources_here, row_count * columns
    )

    def read_nodes(node_ids):
        local_ids = node_ids - first_row * columns
        inside = (local_ids >= 0) & (local_ids < row_count * columns)
        picked = jnp.take_along_axis(
            surface, jnp.clip(local_ids, 0, row_count * columns - 1), axis=1
        )
        return jnp.where(inside, picked, 0.0)

    local_readings = read_nodes(receivers[:, :, 0]) - read_nodes(receivers[:, :, 1])
    predicted = lax.psum(local_readings, "space")
    misfit = predicted - observed
    adjoint_source = surface_source(
        jnp.concatenate([receivers[:, :, 0], receivers[:, :, 1]], axis=1),
        jnp.concatenate([misfit, -misfit], axis=1),
        base_row,
        span,
        layer_count,
        columns,
    )
    adjoint = chebyshev(
        adjoint_init, adjoint_source, face_terms, diagonal, inverse, local_pad, inside_rows
    )
    forward_pad = forward[:, :, margin_rows - 1 : margin_rows + row_count + 1, :]
    adjoint_pad = adjoint[:, :, margin_rows - 1 : margin_rows + row_count + 1, :]
    local_terms = jnp.sum(sensitivity(forward_pad, adjoint_pad), axis=0)
    summed = lax.psum(local_terms, "src")
    share = columns // lax.axis_size("src")
    return lax.dynamic_slice_in_dim(summed, lax.axis_index("src") * share, share, 2)


def solution(mesh):
    return jax.shard_map(
        per_device,
        mesh=mesh,
        in_specs=(
            P("src", None, "space", None),
            P("src", None, "space", None),
            P(None, "space", "src"),
            P("src", None),
            P("src", None, None),
            P("src", None),
        ),
        out_specs=P(None, "space", "src"),
        check_vma=False,
    )
```

profile of v0, /device:TPU:0, one launch (start us, length us, event | category | flops | bytes accessed | tf_op | source)
XLA Modules:
  0.0 187.9 jit_solution(12918429776498886450)
XLA Ops:
  6.5 16.0 %all_gather.3 = f32[4,16,1024]{2,1,0:T(8,128)S(1)} all-gather(f32[4,16,256]{2,1,0:T(8,128)} %param.11), channel_id=1, replica_groups=mesh['space'=8,'src'=4] {'src'}, dimensions={2}, use_global_device_ids=true | all-gather | bytes 327680 | tf_op jit(solution)/shard_map/all_gather | solution.py:137
  22.6 1.3 collective-permute-start.2
  25.2 2.3 %fusion.150 = (f32[4,4,5,1024]{3,2,0,1:T(8,128)}, f32[4,4,5,1024]{3,2,0,1:T(8,128)}) fusion(f32[4,4,16,1024]{3,2,1,0:T(8,128)} %param.9), kind=kLoop, calls=%fused_computation.233 | loop fusion | bytes 1703936 | tf_op jit(solution)/shard_map/slice | solution.py:20
  27.5 5.6 %collective-permute-start = (f32[4,4,5,1024]{3,2,0,1:T(8,128)}, f32[4,4,5,1024]{3,2,0,1:T(8,128)}, u32[]{:S(2)}, u32[]{:S(2)}) collective-permute-start(f32[4,4,5,1024]{3,2,0,1:T(8,128)} %get-tuple-element.28), channel_id=1, source_target_pairs={{0,4},{4,8},{8,12},{12,16},{16,20},{20,24},{24,28},{1,5},{5,9},{9,... | collective-permute-start | bytes 983048 | tf_op jit(solution)/shard_map/ppermute | solution.py:19
  35.5 4.3 %collective-permute-start.4 = (f32[4,4,5,1024]{3,2,0,1:T(8,128)}, f32[4,4,5,1024]{3,2,0,1:T(8,128)}, u32[]{:S(2)}, u32[]{:S(2)}) collective-permute-start(f32[4,4,5,1024]{3,2,0,1:T(8,128)} %get-tuple-element.26), channel_id=1, source_target_pairs={{0,4},{4,8},{8,12},{12,16},{16,20},{20,24},{24,28},{1,5},{5,9},{9,... | collective-permute-start | bytes 983048 | tf_op jit(solution)/shard_map/ppermute | solution.py:19
  46.1 2.2 %pad_maximum_fusion = f32[4,4,26,1024]{3,2,0,1:T(8,128)S(1)} fusion(f32[4,4,5,1024]{3,2,0,1:T(8,128)} %collective-permute-done.1, f32[4,4,5,1024]{3,2,0,1:T(8,128)} %collective-permute-done, f32[4,4,16,1024]{3,2,1,0:T(8,128)S(1)} %copy-done.8), kind=kLoop, calls=%fused_computation.130 | loop fusion | flops 851968 | bytes 3407872 | tf_op jit(solution)/shard_map/concatenate | solution.py:23
  48.3 2.6 %multiply_multiply_fusion.1 = (f32[4,4,26,1024]{3,2,0,1:T(8,128)S(1)}, f32[4,4,26,1024]{3,2,0,1:T(8,128)S(1)}) fusion(f32[4,26,1024]{2,1,0:T(8,128)S(1)} %get-tuple-element.15, f32[26]{0:T(128)S(1)} %and_convert_fusion, f32[4,26,1024]{2,1,0:T(8,128)S(1)} %get-tuple-element.31, f32[4,4,26,1024]{3,2,0,1:T(8,128)S(1)} %pad_maximum_fusion, ...), kind=kLoop, calls=%fused_computation.137 | loop fusion | flops 7241728 | bytes 8945768 | tf_op jit(solution)/shard_map/div | solution.py:75
  50.9 2.8 %multiply_add_fusion.3 = (f32[4,4,26,1024]{3,2,0,1:T(8,128)S(1)}, f32[4,4,26,1024]{3,2,0,1:T(8,128)S(1)}) fusion(f32[4,4,26,1024]{3,2,0,1:T(8,128)S(1)} %get-tuple-element.23, f32[4,26,1024]{2,1,0:T(8,128)S(1)} %get-tuple-element.41, f32[4,26,1024]{2,1,0:T(8,128)S(1)} %get-tuple-element.15, f32[26]{0:T(128)S(1)} %and_convert_fusion, ...), kind=kLoop, calls=%fused_computation.135 | loop fusion | flops 8093696 | bytes 10649704 | tf_op jit(solution)/shard_map/add | solution.py:85
  53.7 3.1 %multiply_add_fusion.2 = (f32[4,4,26,1024]{3,2,0,1:T(8,128)S(1)}, f32[4,4,26,1024]{3,2,0,1:T(8,128)S(1)}) fusion(f32[4,26,1024]{2,1,0:T(8,128)S(1)} %get-tuple-element.40, f32[4,4,26,1024]{3,2,0,1:T(8,128)S(1)} %get-tuple-element.21, f32[4,26,1024]{2,1,0:T(8,128)S(1)} %get-tuple-element.41, f32[4,4,26,1024]{3,2,0,1:T(8,128)S(1)} %get-tuple-element.23, ...), kind=kLoop, calls=%fused_computation.134 | loop fusion | flops 9371648 | bytes 12779624 | tf_op jit(solution)/shard_map/add | solution.py:85
  56.9 4.9 %fusion.37 = f32[4,4,26,1024]{3,2,0,1:T(8,128)S(1)} fusion(f32[4,4,26,1024]{3,2,0,1:T(8,128)S(1)} %get-tuple-element.19, f32[4,4,26,1024]{3,2,0,1:T(8,128)S(1)} %get-tuple-element.18, f32[4,4,26,1024]{3,2,0,1:T(8,128)S(1)} %get-tuple-element.23, f32[4,26,1024]{2,1,0:T(8,128)S(1)} %get-tuple-element.14, f32[26]{0:T(128)S(1)} %and_convert_fusion, ...), kind=kLoop, calls=%fused_computation.73 | loop fusion | flops 12353536 | bytes 14483560 | tf_op jit(solution)/shard_map/add | solution.py:79
  64.5 1.5 gather_fusion
  66.1 1.5 gather_fusion.1
  67.8 16.1 %psum.14 = f32[4,32]{1,0:T(4,128)S(1)} all-reduce(f32[4,32]{1,0:T(4,128)S(1)} %fusion.136), channel_id=1, replica_groups=mesh['space'=8,'src'=4] {'space'}, use_global_device_ids=true, to_apply=%region_1.3 | all-reduce | flops 128 | bytes 1024 | tf_op jit(solution)/shard_map/psum | solution.py:172
  84.9 35.8 %scatter_fusion.1 = f32[4,26624]{1,0:T(4,128)} fusion(f32[4,26624]{1,0:T(4,128)} %broadcast.247, s32[256]{0:T(256)S(1)} %reshape.118, f32[256]{0:T(256)S(1)} %reshape.120), kind=kCustom, calls=%fused_computation.3 | custom fusion | flops 256 | bytes 5120 | tf_op jit(solution)/shard_map/scatter-add | solution.py:127
  120.7 2.2 %reshape.98 = f32[4,1,26,1024]{3,2,0,1:T(8,128)} reshape(f32[4,26624]{1,0:T(4,128)} %scatter_fusion.1) | data formatting | bytes 851968 | tf_op jit(solution)/shard_map/reshape | solution.py:129
  122.9 2.0 %pad_maximum_fusion.1 = f32[4,4,26,1024]{3,2,0,1:T(8,128)S(1)} fusion(f32[4,4,5,1024]{3,2,0,1:T(8,128)} %collective-permute-done.5, f32[4,4,5,1024]{3,2,0,1:T(8,128)} %collective-permute-done.4, f32[4,4,16,1024]{3,2,1,0:T(8,128)} %param.10), kind=kLoop, calls=%fused_computation.131 | loop fusion | flops 851968 | bytes 3407872 | tf_op jit(solution)/shard_map/concatenate | solution.py:23
  124.9 2.6 %multiply_multiply_fusion = (f32[4,4,26,1024]{3,2,0,1:T(8,128)S(1)}, f32[4,4,26,1024]{3,2,0,1:T(8,128)S(1)}) fusion(f32[4,26,1024]{2,1,0:T(8,128)S(1)} %get-tuple-element.15, f32[26]{0:T(128)S(1)} %and_convert_fusion, f32[4,26,1024]{2,1,0:T(8,128)S(1)} %get-tuple-element.31, f32[4,4,26,1024]{3,2,0,1:T(8,128)S(1)} %pad_maximum_fusion.1, ...), kind=kLoop, calls=%fused_computation.136 | loop fusion | flops 7241728 | bytes 8945768 | tf_op jit(solution)/shard_map/div | solution.py:75
  127.5 2.8 %multiply_add_fusion.1 = (f32[4,4,26,1024]{3,2,0,1:T(8,128)S(1)}, f32[4,4,26,1024]{3,2,0,1:T(8,128)S(1)}) fusion(f32[4,4,26,1024]{3,2,0,1:T(8,128)S(1)} %get-tuple-element.11, f32[4,26,1024]{2,1,0:T(8,128)S(1)} %copy-done.5, f32[4,26,1024]{2,1,0:T(8,128)S(1)} %get-tuple-element.15, f32[26]{0:T(128)S(1)} %and_convert_fusion, ...), kind=kLoop, calls=%fused_computation.133 | loop fusion | flops 8093696 | bytes 10649704 | tf_op jit(solution)/shard_map/add | solution.py:85
  130.3 3.1 %multiply_add_fusion = (f32[4,4,26,1024]{3,2,0,1:T(8,128)S(1)}, f32[4,4,26,1024]{3,2,0,1:T(8,128)S(1)}) fusion(f32[4,26,1024]{2,1,0:T(8,128)S(1)} %copy-done.14, f32[4,4,26,1024]{3,2,0,1:T(8,128)S(1)} %get-tuple-element.9, f32[4,26,1024]{2,1,0:T(8,128)S(1)} %copy-done.5, f32[4,4,26,1024]{3,2,0,1:T(8,128)S(1)} %get-tuple-element.11, ...), kind=kLoop, calls=%fused_computation.132 | loop fusion | flops 9371648 | bytes 12779624 | tf_op jit(solution)/shard_map/add | solution.py:85
  133.5 5.0 %fusion.76 = f32[4,4,26,1024]{3,2,0,1:T(8,128)S(1)} fusion(f32[4,4,26,1024]{3,2,0,1:T(8,128)S(1)} %get-tuple-element.7, f32[4,4,26,1024]{3,2,0,1:T(8,128)S(1)} %get-tuple-element.6, f32[4,4,26,1024]{3,2,0,1:T(8,128)S(1)} %get-tuple-element.11, f32[4,26,1024]{2,1,0:T(8,128)S(1)} %copy-done.12, f32[26]{0:T(128)S(1)} %and_convert_fusion, ...), kind=kLoop, calls=%fused_computation.112 | loop fusion | flops 12353536 | bytes 14483560 | tf_op jit(solution)/shard_map/add | solution.py:79
  138.7 1.4 copy-done.7
  140.1 1.8 fusion.101
  142.7 36.9 %all-reduce.34.cloned.1.call-done = f32[4,16,1024]{2,1,0:T(8,128)} async-done(((f32[4,16,1024]{2,1,0:T(8,128)}), f32[4,16,1024]{2,1,0:T(8,128)}) %all-reduce.34.cloned.1.call-update) | async-done | bytes 262160 | tf_op jit(solution)/shard_map/psum | solution.py:188
  179.6 1.5 constant_dynamic-slice_fusion
  (93 shorter events, 14.6 us)
Async XLA Ops:
  6.5 27.8 %copy-start.9 = (f32[4,4,16,1024]{3,2,1,0:T(8,128)S(1)}, f32[4,4,16,1024]{3,2,1,0:T(8,128)}, u32[]{:S(2)}) copy-start(f32[4,4,16,1024]{3,2,1,0:T(8,128)} %param.10) | copy-start | bytes 3145732
  6.5 173.1 %all-reduce.34.cloned.1.call-start = ((), (), s32[]{:S(2)}) async-start(), calls=%async_computation | async-start | bytes 524288 | tf_op jit(solution)/shard_map/psum | solution.py:188
  22.6 20.1 %collective-permute-start.2 = (f32[4,6,1024]{2,1,0:T(8,128)S(1)}, f32[4,6,1024]{2,1,0:T(8,128)S(1)}, u32[]{:S(2)}, u32[]{:S(2)}) collective-permute-start(f32[4,6,1024]{2,1,0:T(8,128)S(1)} %get-tuple-element.36), channel_id=1, source_target_pairs={{0,4},{4,8},{8,12},{12,16},{16,20},{20,24},{24,28},{1,5},{5,9},{9,... | collective-permute-start | bytes 294920 | tf_op jit(solution)/shard_map/ppermute | solution.py:19
  23.9 15.9 %copy-start.20 = (s32[4,2]{0,1:T(2,128)S(1)}, s32[4,2]{0,1:T(2,128)}, u32[]{:S(2)}) copy-start(s32[4,2]{0,1:T(2,128)} %param.12) | copy-start | bytes 100
  23.9 16.1 %copy-start.23 = (f32[2]{0:T(128)S(1)}, f32[2]{0:T(128)}, u32[]{:S(2)}) copy-start(f32[2]{0:T(128)} %constant.30.clone) | copy-start | bytes 28
  23.9 20.1 %collective-permute-start.3 = (f32[4,6,1024]{2,1,0:T(8,128)S(1)}, f32[4,6,1024]{2,1,0:T(8,128)S(1)}, u32[]{:S(2)}, u32[]{:S(2)}) collective-permute-start(f32[4,6,1024]{2,1,0:T(8,128)S(1)} %get-tuple-element.37), channel_id=1, source_target_pairs={{4,0},{8,4},{12,8},{16,12},{20,16},{24,20},{28,24},{5,1},{9,5},{13... | collective-permute-start | bytes 294920 | tf_op jit(solution)/shard_map/ppermute | solution.py:22
  27.5 18.2 %collective-permute-start = (f32[4,4,5,1024]{3,2,0,1:T(8,128)}, f32[4,4,5,1024]{3,2,0,1:T(8,128)}, u32[]{:S(2)}, u32[]{:S(2)}) collective-permute-start(f32[4,4,5,1024]{3,2,0,1:T(8,128)} %get-tuple-element.28), channel_id=1, source_target_pairs={{0,4},{4,8},{8,12},{12,16},{16,20},{20,24},{24,28},{1,5},{5,9},{9,... | collective-permute-start | bytes 983048 | tf_op jit(solution)/shard_map/ppermute | solution.py:19
  33.1 12.6 %collective-permute-start.1 = (f32[4,4,5,1024]{3,2,0,1:T(8,128)}, f32[4,4,5,1024]{3,2,0,1:T(8,128)}, u32[]{:S(2)}, u32[]{:S(2)}) collective-permute-start(f32[4,4,5,1024]{3,2,0,1:T(8,128)} %get-tuple-element.29), channel_id=1, source_target_pairs={{4,0},{8,4},{12,8},{16,12},{20,16},{24,20},{28,24},{5,1},{9,5},{13... | collective-permute-start | bytes 983048 | tf_op jit(solution)/shard_map/ppermute | solution.py:22
  35.5 87.4 %collective-permute-start.4 = (f32[4,4,5,1024]{3,2,0,1:T(8,128)}, f32[4,4,5,1024]{3,2,0,1:T(8,128)}, u32[]{:S(2)}, u32[]{:S(2)}) collective-permute-start(f32[4,4,5,1024]{3,2,0,1:T(8,128)} %get-tuple-element.26), channel_id=1, source_target_pairs={{0,4},{4,8},{8,12},{12,16},{16,20},{20,24},{24,28},{1,5},{5,9},{9,... | collective-permute-start | bytes 983048 | tf_op jit(solution)/shard_map/ppermute | solution.py:19
  42.6 80.2 %collective-permute-start.5 = (f32[4,4,5,1024]{3,2,0,1:T(8,128)}, f32[4,4,5,1024]{3,2,0,1:T(8,128)}, u32[]{:S(2)}, u32[]{:S(2)}) collective-permute-start(f32[4,4,5,1024]{3,2,0,1:T(8,128)} %get-tuple-element.27), channel_id=1, source_target_pairs={{4,0},{8,4},{12,8},{16,12},{20,16},{24,20},{28,24},{5,1},{9,5},{13... | collective-permute-start | bytes 983048 | tf_op jit(solution)/shard_map/ppermute | solution.py:22
  44.6 12.2 %copy-start.11 = (f32[4,26,1024]{2,1,0:T(8,128)}, f32[4,26,1024]{2,1,0:T(8,128)S(1)}, u32[]{:S(2)}) copy-start(f32[4,26,1024]{2,1,0:T(8,128)S(1)} %get-tuple-element.14) | copy-start | bytes 1277956
  45.6 5.3 %copy-start.15 = (f32[4,26,1024]{2,1,0:T(8,128)}, f32[4,26,1024]{2,1,0:T(8,128)S(1)}, u32[]{:S(2)}) copy-start(f32[4,26,1024]{2,1,0:T(8,128)S(1)} %get-tuple-element.24) | copy-start | bytes 1277956
  45.6 8.1 %copy-start.13 = (f32[4,26,1024]{2,1,0:T(8,128)}, f32[4,26,1024]{2,1,0:T(8,128)S(1)}, u32[]{:S(2)}) copy-start(f32[4,26,1024]{2,1,0:T(8,128)S(1)} %get-tuple-element.40) | copy-start | bytes 1277956
  45.6 11.3 %copy-start = (f32[4,26,1024]{2,1,0:T(8,128)}, f32[4,26,1024]{2,1,0:T(8,128)S(1)}, u32[]{:S(2)}) copy-start(f32[4,26,1024]{2,1,0:T(8,128)S(1)} %get-tuple-element.33) | copy-start | bytes 1277956
  45.6 11.3 %copy-start.2 = (f32[4,26,1024]{2,1,0:T(8,128)}, f32[4,26,1024]{2,1,0:T(8,128)S(1)}, u32[]{:S(2)}) copy-start(f32[4,26,1024]{2,1,0:T(8,128)S(1)} %get-tuple-element.25) | copy-start | bytes 1277956
  45.6 11.3 %copy-start.4 = (f32[4,26,1024]{2,1,0:T(8,128)}, f32[4,26,1024]{2,1,0:T(8,128)S(1)}, u32[]{:S(2)}) copy-start(f32[4,26,1024]{2,1,0:T(8,128)S(1)} %get-tuple-element.41) | copy-start | bytes 1277956
  45.6 2.6 %copy-start.18 = (f32[4,1,26,1024]{3,2,0,1:T(8,128)S(1)}, f32[4,1,26,1024]{3,2,0,1:T(8,128)}, u32[]{:S(2)}) copy-start(f32[4,1,26,1024]{3,2,0,1:T(8,128)} %reshape.97) | copy-start | bytes 1277956
  64.5 19.4 %copy-start.22 = (f32[4,32]{1,0:T(4,128)S(1)}, f32[4,32]{1,0:T(4,128)}, u32[]{:S(2)}) copy-start(f32[4,32]{1,0:T(4,128)} %param.14) | copy-start | bytes 1540
  124.9 2.6 %copy-start.5 = (f32[4,26,1024]{2,1,0:T(8,128)S(1)}, f32[4,26,1024]{2,1,0:T(8,128)}, u32[]{:S(2)}) copy-start(f32[4,26,1024]{2,1,0:T(8,128)} %copy-done.4) | copy-start | bytes 1277956
  124.9 2.6 %copy-start.16 = (f32[4,26,1024]{2,1,0:T(8,128)S(1)}, f32[4,26,1024]{2,1,0:T(8,128)}, u32[]{:S(2)}) copy-start(f32[4,26,1024]{2,1,0:T(8,128)} %copy-done.15) | copy-start | bytes 1277956
  127.5 2.8 %copy-start.14 = (f32[4,26,1024]{2,1,0:T(8,128)S(1)}, f32[4,26,1024]{2,1,0:T(8,128)}, u32[]{:S(2)}) copy-start(f32[4,26,1024]{2,1,0:T(8,128)} %copy-done.13) | copy-start | bytes 1277956
  130.3 3.2 %copy-start.10 = (f32[4,4,16,1024]{3,2,1,0:T(8,128)S(1)}, f32[4,4,16,1024]{3,2,1,0:T(8,128)}, u32[]{:S(2)}) copy-start(f32[4,4,16,1024]{3,2,1,0:T(8,128)} %param.10) | copy-start | bytes 3145732
  130.3 3.2 %copy-start.12 = (f32[4,26,1024]{2,1,0:T(8,128)S(1)}, f32[4,26,1024]{2,1,0:T(8,128)}, u32[]{:S(2)}) copy-start(f32[4,26,1024]{2,1,0:T(8,128)} %copy-done.11) | copy-start | bytes 1277956
  133.5 5.2 %copy-start.17 = (f32[4,4,16,1024]{3,2,0,1:T(8,128)S(1)}, f32[4,4,16,1024]{3,2,0,1:T(8,128)}, u32[]{:S(2)}) copy-start(f32[4,4,16,1024]{3,2,0,1:T(8,128)} %slice.345) | copy-start | bytes 3145732
  (7 other events, 12.4 us)
Sparse Core Ops, SparseCore 0:
  142.8 36.7 all-reduce.33
where the time goes:
time: 189 us; the launch traced here: 188 us
  other arithmetic  72.2 us (38%)
  waiting for transfers between devices  36.9 us (20%)
  blocking collectives  32.1 us (17%)
  local copies, waits for them, and re-layouts  17.7 us (9%)
  starting transfers between devices  15 us (8%)
  between operations  14 us (7%)
    psum x1, waiting for transfers between devices, per_device(): summed = lax.psum(local_terms, 'src')  36.9 us
    scatter-add x2, other arithmetic, surface_source(): plane = jnp.zeros((sources_here, span * columns), jnp.float32).at[source_...  36.7 us
    psum x1, blocking collectives, per_device(): predicted = lax.psum(local_readings, 'space')  16.1 us
    all_gather x1, blocking collectives, per_device(): whole_sigma = lax.all_gather(conductivity, 'src', axis=2, tiled=True)  16 us
    add x4, other arithmetic, chebyshev(): factor_next * factor * direction  11.9 us
    ppermute x3, starting transfers between devices, padded_2(): lax.ppermute(lax.slice_in_dim(block, block.shape[dim] - width, None, axis...  11.1 us
    add x2, other arithmetic, chebyshev(): potential = potential + direction  9.93 us
    div x2, other arithmetic, chebyshev(): direction = inverse * residual / THETA  5.15 us
  transfers between devices with their start and end apart: 7, of which 1 were waited for; matrix products, arithmetic and copies ran while one was open for 36% of the time, Pallas kernels for 0%

commit v1 on v0

--- a/solution.py
+++ b/solution.py
@@ -9,6 +9,14 @@
 THETA = 1.025
 DELTA = 0.975
 RATIO = THETA / DELTA
+
+
+def add_in_pairs(x, name):
+    n_dev, acc = (lax.axis_size(name), x)
+    for far in [1 << k for k in range(n_dev.bit_length() - 1)]:
+        swap = [(i, i ^ far) for i in range(n_dev)]
+        acc = acc + lax.ppermute(acc, name, swap)
+    return acc
 
 
 def padded_2(block, sides, width):
@@ -185,7 +193,7 @@
     forward_pad = forward[:, :, margin_rows - 1 : margin_rows + row_count + 1, :]
     adjoint_pad = adjoint[:, :, margin_rows - 1 : margin_rows + row_count + 1, :]
     local_terms = jnp.sum(sensitivity(forward_pad, adjoint_pad), axis=0)
-    summed = lax.psum(local_terms, "src")
+    summed = add_in_pairs(local_terms, "src")
     share = columns // lax.axis_size("src")
     return lax.dynamic_slice_in_dim(summed, lax.axis_index("src") * share, share, 2)
 

time: 189 us -> 157 us (0.83)
  waiting for transfers between devices: 36.9 us -> 14.6 us
  between operations: 14 us -> 0.58 us
  starting transfers between devices: 15 us -> 19.5 us
    psum x1 -> x0, waiting for transfers between devices: 36.9 us -> none  [per_device(): summed = lax.psum(local_terms, 'src')]
    ppermute x0 -> x2, waiting for transfers between devices: none -> 14.6 us  [add_in_pairs(): acc = acc + lax.ppermute(acc, name, swap)]
    ppermute x0 -> x2, starting transfers between devices: none -> 4.46 us  [add_in_pairs(): acc = acc + lax.ppermute(acc, name, swap)]
  transfers between devices with their start and end apart: 7 -> 8, of which waited for: 1 -> 2; matrix products, arithmetic and copies ran while one was open for 36% -> 43% of each run, Pallas kernels for 0% -> 0%
where the time goes in v1:
time: 157 us; the launch traced here: 156 us
  other arithmetic  72.7 us (46%)
  blocking collectives  32.1 us (20%)
  starting transfers between devices  19.5 us (12%)
  local copies, waits for them, and re-layouts  16.3 us (10%)
  waiting for transfers between devices  14.6 us (9%)
    scatter-add x2, other arithmetic, surface_source(): plane = jnp.zeros((sources_here, span * columns), jnp.float32).at[source_...  37.3 us
    psum x1, blocking collectives, per_device(): predicted = lax.psum(local_readings, 'space')  16.1 us
    all_gather x1, blocking collectives, per_device(): whole_sigma = lax.all_gather(conductivity, 'src', axis=2, tiled=True)  16 us
    ppermute x2, waiting for transfers between devices, add_in_pairs(): acc = acc + lax.ppermute(acc, name, swap)  14.6 us
    add x4, other arithmetic, chebyshev(): factor_next * factor * direction  11.8 us
    ppermute x3, starting transfers between devices, padded_2(): lax.ppermute(lax.slice_in_dim(block, block.shape[dim] - width, None, axis...  11.1 us
    add x2, other arithmetic, chebyshev(): potential = potential + direction  9.88 us
    div x2, other arithmetic, chebyshev(): direction = inverse * residual / THETA  5.1 us
  transfers between devices with their start and end apart: 8, of which 2 were waited for; matrix products, arithmetic and copies ran while one was open for 43% of the time, Pallas kernels for 0%

profile of v1, /device:TPU:0, one launch (start us, length us, event | category | flops | bytes accessed | tf_op | source)
XLA Modules:
  0.0 155.7 jit_solution(9272554581398346421)
XLA Ops:
  0.0 16.0 %all_gather.3 = f32[4,16,1024]{2,1,0:T(8,128)S(1)} all-gather(f32[4,16,256]{2,1,0:T(8,128)} %param.11), channel_id=1, replica_groups=mesh['space'=8,'src'=4] {'src'}, dimensions={2}, use_global_device_ids=true | all-gather | bytes 327680 | tf_op jit(solution)/shard_map/all_gather | solution.py:145
  18.6 2.3 %fusion.150 = (f32[4,4,5,1024]{3,2,0,1:T(8,128)}, f32[4,4,5,1024]{3,2,0,1:T(8,128)}) fusion(f32[4,4,16,1024]{3,2,1,0:T(8,128)} %param.9), kind=kLoop, calls=%fused_computation.234 | loop fusion | bytes 1703936 | tf_op jit(solution)/shard_map/slice | solution.py:28
  20.9 5.6 %collective-permute-start = (f32[4,4,5,1024]{3,2,0,1:T(8,128)}, f32[4,4,5,1024]{3,2,0,1:T(8,128)}, u32[]{:S(2)}, u32[]{:S(2)}) collective-permute-start(f32[4,4,5,1024]{3,2,0,1:T(8,128)} %get-tuple-element.28), channel_id=1, source_target_pairs={{0,4},{4,8},{8,12},{12,16},{16,20},{20,24},{24,28},{1,5},{5,9},{9,... | collective-permute-start | bytes 983048 | tf_op jit(solution)/shard_map/ppermute | solution.py:27
  28.9 4.3 %collective-permute-start.4 = (f32[4,4,5,1024]{3,2,0,1:T(8,128)}, f32[4,4,5,1024]{3,2,0,1:T(8,128)}, u32[]{:S(2)}, u32[]{:S(2)}) collective-permute-start(f32[4,4,5,1024]{3,2,0,1:T(8,128)} %get-tuple-element.26), channel_id=1, source_target_pairs={{0,4},{4,8},{8,12},{12,16},{16,20},{20,24},{24,28},{1,5},{5,9},{9,... | collective-permute-start | bytes 983048 | tf_op jit(solution)/shard_map/ppermute | solution.py:27
  39.5 2.2 %pad_maximum_fusion = f32[4,4,26,1024]{3,2,0,1:T(8,128)S(1)} fusion(f32[4,4,5,1024]{3,2,0,1:T(8,128)} %collective-permute-done.1, f32[4,4,5,1024]{3,2,0,1:T(8,128)} %collective-permute-done, f32[4,4,16,1024]{3,2,1,0:T(8,128)S(1)} %copy-done.8), kind=kLoop, calls=%fused_computation.130 | loop fusion | flops 851968 | bytes 3407872 | tf_op jit(solution)/shard_map/concatenate | solution.py:31
  41.8 2.5 %multiply_multiply_fusion.1 = (f32[4,4,26,1024]{3,2,0,1:T(8,128)S(1)}, f32[4,4,26,1024]{3,2,0,1:T(8,128)S(1)}) fusion(f32[4,26,1024]{2,1,0:T(8,128)S(1)} %get-tuple-element.15, f32[26]{0:T(128)S(1)} %and_convert_fusion, f32[4,26,1024]{2,1,0:T(8,128)S(1)} %get-tuple-element.31, f32[4,4,26,1024]{3,2,0,1:T(8,128)S(1)} %pad_maximum_fusion, ...), kind=kLoop, calls=%fused_computation.137 | loop fusion | flops 7241728 | bytes 8945768 | tf_op jit(solution)/shard_map/div | solution.py:83
  44.3 2.7 %multiply_add_fusion.3 = (f32[4,4,26,1024]{3,2,0,1:T(8,128)S(1)}, f32[4,4,26,1024]{3,2,0,1:T(8,128)S(1)}) fusion(f32[4,4,26,1024]{3,2,0,1:T(8,128)S(1)} %get-tuple-element.23, f32[4,26,1024]{2,1,0:T(8,128)S(1)} %get-tuple-element.41, f32[4,26,1024]{2,1,0:T(8,128)S(1)} %get-tuple-element.15, f32[26]{0:T(128)S(1)} %and_convert_fusion, ...), kind=kLoop, calls=%fused_computation.135 | loop fusion | flops 8093696 | bytes 10649704 | tf_op jit(solution)/shard_map/add | solution.py:93
  47.1 3.2 %multiply_add_fusion.2 = (f32[4,4,26,1024]{3,2,0,1:T(8,128)S(1)}, f32[4,4,26,1024]{3,2,0,1:T(8,128)S(1)}) fusion(f32[4,26,1024]{2,1,0:T(8,128)S(1)} %get-tuple-element.40, f32[4,4,26,1024]{3,2,0,1:T(8,128)S(1)} %get-tuple-element.21, f32[4,26,1024]{2,1,0:T(8,128)S(1)} %get-tuple-element.41, f32[4,4,26,1024]{3,2,0,1:T(8,128)S(1)} %get-tuple-element.23, ...), kind=kLoop, calls=%fused_computation.134 | loop fusion | flops 9371648 | bytes 12779624 | tf_op jit(solution)/shard_map/add | solution.py:93
  50.3 4.9 %fusion.37 = f32[4,4,26,1024]{3,2,0,1:T(8,128)S(1)} fusion(f32[4,4,26,1024]{3,2,0,1:T(8,128)S(1)} %get-tuple-element.19, f32[4,4,26,1024]{3,2,0,1:T(8,128)S(1)} %get-tuple-element.18, f32[4,4,26,1024]{3,2,0,1:T(8,128)S(1)} %get-tuple-element.23, f32[4,26,1024]{2,1,0:T(8,128)S(1)} %get-tuple-element.14, f32[26]{0:T(128)S(1)} %and_convert_fusion, ...), kind=kLoop, calls=%fused_computation.73 | loop fusion | flops 12353536 | bytes 14483560 | tf_op jit(solution)/shard_map/add | solution.py:87
  57.9 1.5 gather_fusion
  59.5 1.5 gather_fusion.1
  61.2 16.1 %psum.7 = f32[4,32]{1,0:T(4,128)S(1)} all-reduce(f32[4,32]{1,0:T(4,128)S(1)} %fusion.136), channel_id=1, replica_groups=mesh['space'=8,'src'=4] {'space'}, use_global_device_ids=true, to_apply=%region_1.3 | all-reduce | flops 128 | bytes 1024 | tf_op jit(solution)/shard_map/psum | solution.py:180
  78.2 36.5 %scatter_fusion.1 = f32[4,26624]{1,0:T(4,128)} fusion(f32[4,26624]{1,0:T(4,128)} %broadcast.247, s32[256]{0:T(256)S(1)} %reshape.118, f32[256]{0:T(256)S(1)} %reshape.120), kind=kCustom, calls=%fused_computation.3 | custom fusion | flops 256 | bytes 5120 | tf_op jit(solution)/shard_map/scatter-add | solution.py:135
  114.7 2.2 %reshape.98 = f32[4,1,26,1024]{3,2,0,1:T(8,128)} reshape(f32[4,26624]{1,0:T(4,128)} %scatter_fusion.1) | data formatting | bytes 851968 | tf_op jit(solution)/shard_map/reshape | solution.py:137
  116.9 2.0 %pad_maximum_fusion.1 = f32[4,4,26,1024]{3,2,0,1:T(8,128)S(1)} fusion(f32[4,4,5,1024]{3,2,0,1:T(8,128)} %collective-permute-done.5, f32[4,4,5,1024]{3,2,0,1:T(8,128)} %collective-permute-done.4, f32[4,4,16,1024]{3,2,1,0:T(8,128)} %param.10), kind=kLoop, calls=%fused_computation.131 | loop fusion | flops 851968 | bytes 3407872 | tf_op jit(solution)/shard_map/concatenate | solution.py:31
  118.9 2.6 %multiply_multiply_fusion = (f32[4,4,26,1024]{3,2,0,1:T(8,128)S(1)}, f32[4,4,26,1024]{3,2,0,1:T(8,128)S(1)}) fusion(f32[4,26,1024]{2,1,0:T(8,128)S(1)} %get-tuple-element.15, f32[26]{0:T(128)S(1)} %and_convert_fusion, f32[4,26,1024]{2,1,0:T(8,128)S(1)} %get-tuple-element.31, f32[4,4,26,1024]{3,2,0,1:T(8,128)S(1)} %pad_maximum_fusion.1, ...), kind=kLoop, calls=%fused_computation.136 | loop fusion | flops 7241728 | bytes 8945768 | tf_op jit(solution)/shard_map/div | solution.py:83
  121.5 2.7 %multiply_add_fusion.1 = (f32[4,4,26,1024]{3,2,0,1:T(8,128)S(1)}, f32[4,4,26,1024]{3,2,0,1:T(8,128)S(1)}) fusion(f32[4,4,26,1024]{3,2,0,1:T(8,128)S(1)} %get-tuple-element.11, f32[4,26,1024]{2,1,0:T(8,128)S(1)} %copy-done.5, f32[4,26,1024]{2,1,0:T(8,128)S(1)} %get-tuple-element.15, f32[26]{0:T(128)S(1)} %and_convert_fusion, ...), kind=kLoop, calls=%fused_computation.133 | loop fusion | flops 8093696 | bytes 10649704 | tf_op jit(solution)/shard_map/add | solution.py:93
  124.3 3.2 %multiply_add_fusion = (f32[4,4,26,1024]{3,2,0,1:T(8,128)S(1)}, f32[4,4,26,1024]{3,2,0,1:T(8,128)S(1)}) fusion(f32[4,26,1024]{2,1,0:T(8,128)S(1)} %copy-done.14, f32[4,4,26,1024]{3,2,0,1:T(8,128)S(1)} %get-tuple-element.9, f32[4,26,1024]{2,1,0:T(8,128)S(1)} %copy-done.5, f32[4,4,26,1024]{3,2,0,1:T(8,128)S(1)} %get-tuple-element.11, ...), kind=kLoop, calls=%fused_computation.132 | loop fusion | flops 9371648 | bytes 12779624 | tf_op jit(solution)/shard_map/add | solution.py:93
  127.5 5.0 %fusion.76 = f32[4,4,26,1024]{3,2,0,1:T(8,128)S(1)} fusion(f32[4,4,26,1024]{3,2,0,1:T(8,128)S(1)} %get-tuple-element.7, f32[4,4,26,1024]{3,2,0,1:T(8,128)S(1)} %get-tuple-element.6, f32[4,4,26,1024]{3,2,0,1:T(8,128)S(1)} %get-tuple-element.11, f32[4,26,1024]{2,1,0:T(8,128)S(1)} %copy-done.12, f32[26]{0:T(128)S(1)} %and_convert_fusion, ...), kind=kLoop, calls=%fused_computation.112 | loop fusion | flops 12353536 | bytes 14483560 | tf_op jit(solution)/shard_map/add | solution.py:87
  134.1 1.8 %fusion.101 = f32[4,16,1024]{2,1,0:T(8,128)S(1)} fusion(f32[4,4,16,1024]{3,2,0,1:T(8,128)S(1)} %copy-done.17, f32[4,4,16,1024]{3,2,0,1:T(8,128)S(1)} %slice.349, f32[4,4,26,1024]{3,2,0,1:T(8,128)S(1)} %fusion.76, f32[4,4,26,1024]{3,2,0,1:T(8,128)S(1)} %copy-done.7), kind=kLoop, calls=%fused_computation.153 | loop fusion | flops 8585216 | bytes 6553600 | tf_op jit(solution)/shard_map/reduce_sum | solution.py:195
  136.0 1.6 %collective-permute-start.6 = (f32[4,16,1024]{2,1,0:T(8,128)S(1)}, f32[4,16,1024]{2,1,0:T(8,128)S(1)}, u32[]{:S(2)}, u32[]{:S(2)}) collective-permute-start(f32[4,16,1024]{2,1,0:T(8,128)S(1)} %neg.7), channel_id=1, source_target_pairs={{0,1},{1,0},{2,3},{3,2},{4,5},{5,4},{6,7},{7,6},{8,9},{9,8},{10,11... | collective-permute-start | bytes 786440 | tf_op jit(solution)/shard_map/ppermute | solution.py:18
  137.5 4.9 %collective-permute-done.6 = f32[4,16,1024]{2,1,0:T(8,128)S(1)} collective-permute-done((f32[4,16,1024]{2,1,0:T(8,128)S(1)}, f32[4,16,1024]{2,1,0:T(8,128)S(1)}, u32[]{:S(2)}, u32[]{:S(2)}) %collective-permute-start.6) | collective-permute-done | bytes 262176 | tf_op jit(solution)/shard_map/ppermute | solution.py:18
  142.4 2.9 %collective-permute-start.7 = (f32[4,16,1024]{2,1,0:T(8,128)S(1)}, f32[4,16,1024]{2,1,0:T(8,128)S(1)}, u32[]{:S(2)}, u32[]{:S(2)}) collective-permute-start(f32[4,16,1024]{2,1,0:T(8,128)S(1)} %negate_add_fusion), channel_id=1, source_target_pairs={{0,2},{1,3},{2,0},{3,1},{4,6},{5,7},{6,4},{7,5},{8,10},{9,11},{10,... | collective-permute-start | bytes 786440 | tf_op jit(solution)/shard_map/ppermute | solution.py:18
  145.3 9.7 %collective-permute-done.7 = f32[4,16,1024]{2,1,0:T(8,128)S(1)} collective-permute-done((f32[4,16,1024]{2,1,0:T(8,128)S(1)}, f32[4,16,1024]{2,1,0:T(8,128)S(1)}, u32[]{:S(2)}, u32[]{:S(2)}) %collective-permute-start.7) | collective-permute-done | bytes 262176 | tf_op jit(solution)/shard_map/ppermute | solution.py:18
  (95 shorter events, 17.3 us)
Async XLA Ops:
  0.0 27.8 %copy-start.9 = (f32[4,4,16,1024]{3,2,1,0:T(8,128)S(1)}, f32[4,4,16,1024]{3,2,1,0:T(8,128)}, u32[]{:S(2)}) copy-start(f32[4,4,16,1024]{3,2,1,0:T(8,128)} %param.10) | copy-start | bytes 3145732
  16.0 20.1 %collective-permute-start.2 = (f32[4,6,1024]{2,1,0:T(8,128)S(1)}, f32[4,6,1024]{2,1,0:T(8,128)S(1)}, u32[]{:S(2)}, u32[]{:S(2)}) collective-permute-start(f32[4,6,1024]{2,1,0:T(8,128)S(1)} %get-tuple-element.36), channel_id=1, source_target_pairs={{0,4},{4,8},{8,12},{12,16},{16,20},{20,24},{24,28},{1,5},{5,9},{9,... | collective-permute-start | bytes 294920 | tf_op jit(solution)/shard_map/ppermute | solution.py:27
  17.3 15.9 %copy-start.20 = (s32[4,2]{0,1:T(2,128)S(1)}, s32[4,2]{0,1:T(2,128)}, u32[]{:S(2)}) copy-start(s32[4,2]{0,1:T(2,128)} %param.12) | copy-start | bytes 100
  17.3 16.1 %copy-start.23 = (f32[2]{0:T(128)S(1)}, f32[2]{0:T(128)}, u32[]{:S(2)}) copy-start(f32[2]{0:T(128)} %constant.30.clone) | copy-start | bytes 28
  17.3 20.1 %collective-permute-start.3 = (f32[4,6,1024]{2,1,0:T(8,128)S(1)}, f32[4,6,1024]{2,1,0:T(8,128)S(1)}, u32[]{:S(2)}, u32[]{:S(2)}) collective-permute-start(f32[4,6,1024]{2,1,0:T(8,128)S(1)} %get-tuple-element.37), channel_id=1, source_target_pairs={{4,0},{8,4},{12,8},{16,12},{20,16},{24,20},{28,24},{5,1},{9,5},{13... | collective-permute-start | bytes 294920 | tf_op jit(solution)/shard_map/ppermute | solution.py:30
  20.9 18.2 %collective-permute-start = (f32[4,4,5,1024]{3,2,0,1:T(8,128)}, f32[4,4,5,1024]{3,2,0,1:T(8,128)}, u32[]{:S(2)}, u32[]{:S(2)}) collective-permute-start(f32[4,4,5,1024]{3,2,0,1:T(8,128)} %get-tuple-element.28), channel_id=1, source_target_pairs={{0,4},{4,8},{8,12},{12,16},{16,20},{20,24},{24,28},{1,5},{5,9},{9,... | collective-permute-start | bytes 983048 | tf_op jit(solution)/shard_map/ppermute | solution.py:27
  26.5 12.6 %collective-permute-start.1 = (f32[4,4,5,1024]{3,2,0,1:T(8,128)}, f32[4,4,5,1024]{3,2,0,1:T(8,128)}, u32[]{:S(2)}, u32[]{:S(2)}) collective-permute-start(f32[4,4,5,1024]{3,2,0,1:T(8,128)} %get-tuple-element.29), channel_id=1, source_target_pairs={{4,0},{8,4},{12,8},{16,12},{20,16},{24,20},{28,24},{5,1},{9,5},{13... | collective-permute-start | bytes 983048 | tf_op jit(solution)/shard_map/ppermute | solution.py:30
  28.9 88.0 %collective-permute-start.4 = (f32[4,4,5,1024]{3,2,0,1:T(8,128)}, f32[4,4,5,1024]{3,2,0,1:T(8,128)}, u32[]{:S(2)}, u32[]{:S(2)}) collective-permute-start(f32[4,4,5,1024]{3,2,0,1:T(8,128)} %get-tuple-element.26), channel_id=1, source_target_pairs={{0,4},{4,8},{8,12},{12,16},{16,20},{20,24},{24,28},{1,5},{5,9},{9,... | collective-permute-start | bytes 983048 | tf_op jit(solution)/shard_map/ppermute | solution.py:27
  36.1 80.8 %collective-permute-start.5 = (f32[4,4,5,1024]{3,2,0,1:T(8,128)}, f32[4,4,5,1024]{3,2,0,1:T(8,128)}, u32[]{:S(2)}, u32[]{:S(2)}) collective-permute-start(f32[4,4,5,1024]{3,2,0,1:T(8,128)} %get-tuple-element.27), channel_id=1, source_target_pairs={{4,0},{8,4},{12,8},{16,12},{20,16},{24,20},{28,24},{5,1},{9,5},{13... | collective-permute-start | bytes 983048 | tf_op jit(solution)/shard_map/ppermute | solution.py:30
  38.1 12.2 %copy-start.11 = (f32[4,26,1024]{2,1,0:T(8,128)}, f32[4,26,1024]{2,1,0:T(8,128)S(1)}, u32[]{:S(2)}) copy-start(f32[4,26,1024]{2,1,0:T(8,128)S(1)} %get-tuple-element.14) | copy-start | bytes 1277956
  39.1 5.3 %copy-start.15 = (f32[4,26,1024]{2,1,0:T(8,128)}, f32[4,26,1024]{2,1,0:T(8,128)S(1)}, u32[]{:S(2)}) copy-start(f32[4,26,1024]{2,1,0:T(8,128)S(1)} %get-tuple-element.24) | copy-start | bytes 1277956
  39.1 8.0 %copy-start.13 = (f32[4,26,1024]{2,1,0:T(8,128)}, f32[4,26,1024]{2,1,0:T(8,128)S(1)}, u32[]{:S(2)}) copy-start(f32[4,26,1024]{2,1,0:T(8,128)S(1)} %get-tuple-element.40) | copy-start | bytes 1277956
  39.1 11.2 %copy-start = (f32[4,26,1024]{2,1,0:T(8,128)}, f32[4,26,1024]{2,1,0:T(8,128)S(1)}, u32[]{:S(2)}) copy-start(f32[4,26,1024]{2,1,0:T(8,128)S(1)} %get-tuple-element.33) | copy-start | bytes 1277956
  39.1 11.2 %copy-start.2 = (f32[4,26,1024]{2,1,0:T(8,128)}, f32[4,26,1024]{2,1,0:T(8,128)S(1)}, u32[]{:S(2)}) copy-start(f32[4,26,1024]{2,1,0:T(8,128)S(1)} %get-tuple-element.25) | copy-start | bytes 1277956
  39.1 11.2 %copy-start.4 = (f32[4,26,1024]{2,1,0:T(8,128)}, f32[4,26,1024]{2,1,0:T(8,128)S(1)}, u32[]{:S(2)}) copy-start(f32[4,26,1024]{2,1,0:T(8,128)S(1)} %get-tuple-element.41) | copy-start | bytes 1277956
  39.1 2.6 %copy-start.18 = (f32[4,1,26,1024]{3,2,0,1:T(8,128)S(1)}, f32[4,1,26,1024]{3,2,0,1:T(8,128)}, u32[]{:S(2)}) copy-start(f32[4,1,26,1024]{3,2,0,1:T(8,128)} %reshape.97) | copy-start | bytes 1277956
  57.9 19.4 %copy-start.22 = (f32[4,32]{1,0:T(4,128)S(1)}, f32[4,32]{1,0:T(4,128)}, u32[]{:S(2)}) copy-start(f32[4,32]{1,0:T(4,128)} %param.14) | copy-start | bytes 1540
  118.9 2.6 %copy-start.5 = (f32[4,26,1024]{2,1,0:T(8,128)S(1)}, f32[4,26,1024]{2,1,0:T(8,128)}, u32[]{:S(2)}) copy-start(f32[4,26,1024]{2,1,0:T(8,128)} %copy-done.4) | copy-start | bytes 1277956
  121.5 2.8 %copy-start.14 = (f32[4,26,1024]{2,1,0:T(8,128)S(1)}, f32[4,26,1024]{2,1,0:T(8,128)}, u32[]{:S(2)}) copy-start(f32[4,26,1024]{2,1,0:T(8,128)} %copy-done.13) | copy-start | bytes 1277956
  124.3 3.2 %copy-start.10 = (f32[4,4,16,1024]{3,2,1,0:T(8,128)S(1)}, f32[4,4,16,1024]{3,2,1,0:T(8,128)}, u32[]{:S(2)}) copy-start(f32[4,4,16,1024]{3,2,1,0:T(8,128)} %param.10) | copy-start | bytes 3145732
  124.3 3.2 %copy-start.12 = (f32[4,26,1024]{2,1,0:T(8,128)S(1)}, f32[4,26,1024]{2,1,0:T(8,128)}, u32[]{:S(2)}) copy-start(f32[4,26,1024]{2,1,0:T(8,128)} %copy-done.11) | copy-start | bytes 1277956
  127.5 5.2 %copy-start.17 = (f32[4,4,16,1024]{3,2,0,1:T(8,128)S(1)}, f32[4,4,16,1024]{3,2,0,1:T(8,128)}, u32[]{:S(2)}) copy-start(f32[4,4,16,1024]{3,2,0,1:T(8,128)} %slice.345) | copy-start | bytes 3145732
  136.0 6.4 %collective-permute-start.6 = (f32[4,16,1024]{2,1,0:T(8,128)S(1)}, f32[4,16,1024]{2,1,0:T(8,128)S(1)}, u32[]{:S(2)}, u32[]{:S(2)}) collective-permute-start(f32[4,16,1024]{2,1,0:T(8,128)S(1)} %neg.7), channel_id=1, source_target_pairs={{0,1},{1,0},{2,3},{3,2},{4,5},{5,4},{6,7},{7,6},{8,9},{9,8},{10,11... | collective-permute-start | bytes 786440 | tf_op jit(solution)/shard_map/ppermute | solution.py:18
  142.4 12.6 %collective-permute-start.7 = (f32[4,16,1024]{2,1,0:T(8,128)S(1)}, f32[4,16,1024]{2,1,0:T(8,128)S(1)}, u32[]{:S(2)}, u32[]{:S(2)}) collective-permute-start(f32[4,16,1024]{2,1,0:T(8,128)S(1)} %negate_add_fusion), channel_id=1, source_target_pairs={{0,2},{1,3},{2,0},{3,1},{4,6},{5,7},{6,4},{7,5},{8,10},{9,11},{10,... | collective-permute-start | bytes 786440 | tf_op jit(solution)/shard_map/ppermute | solution.py:18
  (8 other events, 15.0 us)
